TPU v7x, 32 devices: a whole 2x2x4 slice. The times are simulated.
32 devices in a mesh: tm: 4 (over z), space: 8 (over y, x, core).
Axes of the slice: x: 2, y: 2, z: 4, core: 2. Of those that a mesh axis runs over, the one named last changes fastest.
Arguments:
- frames: bfloat16 [4, 96, 32, 1280], P('tm', None, 'space'), may hold values from -6 to 6
- cache: bfloat16 [2, 96, 32, 1280], P(None, 'tm', 'space'), may hold values from -6 to 6
- grad_out: bfloat16 [4, 96, 32, 1280], P('tm', None, 'space'), may hold values from -6 to 6
- weight: bfloat16 [3, 3, 3, 96, 96], replicated, may hold values from -0.125 to 0.125
Outputs:
- input_grad: bfloat16 [4, 96, 32, 1280], P('tm', None, 'space')
- cache_grad: bfloat16 [2, 96, 32, 1280], P(None, 'tm', 'space')
- weight_grad: float32 [3, 3, 3, 96, 96], replicated
All inputs are finite; a program needn't handle non-finite values.
Results may differ from a plain program's by a relative error of at most 0.0041.
Values may be sent and summed in bfloat16 or wider, within the bound.
A program may use at most 64 MiB of HBM per device.

v0:
```python
import math

import jax
import jax.numpy as jnp
from jax import lax
from jax.sharding import PartitionSpec as P


def passed_along(value, axis, steps):
    count = lax.axis_size(axis)
    initial, last = (max(0, -steps), min(count, count - steps))
    return lax.ppermute(value, axis, [(source, source + steps) for source in range(initial, last)])


def padded_2(cells, sides, width):
    for axis, dim in sides:
        count = lax.axis_size(axis)
        ends = count - 1
        head = lax.slice_in_dim(cells, 0, width, axis=dim)
        tail = lax.slice_in_dim(cells, cells.shape[dim] - width, cells.shape[dim], axis=dim)
        cells = jnp.concatenate(
            [
                lax.ppermute(tail, axis, [(i, (i + 1) % count) for i in range(ends)]),
                cells,
                lax.ppermute(head, axis, [((i + 1) % count, i) for i in range(ends)]),
            ],
            axis=dim,
        )
    return cells


def per_device(frames, cache, grad_out, weight):
    group_index = lax.axis_index("tm")
    channels = frames.shape[1]
    row_count = frames.shape[2]
    col_count = frames.shape[3]
    prev_one = passed_along(frames, "tm", 1)
    prev_two = passed_along(prev_one, "tm", 1)
    cache_full = lax.all_gather(cache, "tm", axis=1, tiled=True)
    near_frame = jnp.where(group_index >= 1, prev_one[0], cache_full[1])
    far_frame = jnp.where(
        group_index >= 2, prev_two[0], jnp.where(group_index == 1, cache_full[1], cache_full[0])
    )
    window = jnp.stack([far_frame, near_frame, frames[0], grad_out[0]], axis=0)
    padded = padded_2(window, (("space", 2),), 1)
    padded = jnp.pad(padded, ((0, 0), (0, 0), (0, 0), (1, 1)))
    input_pad = padded[:3]
    output_pad = padded[3]
    grad_rows = grad_out[0]
    slices = jnp.stack(
        [
            output_pad[
                :, 2 - row_tap : 2 - row_tap + row_count, 2 - col_tap : 2 - col_tap + col_count
            ]
            for row_tap in range(3)
            for col_tap in range(3)
        ],
        axis=0,
    )
    tap_weights = jnp.transpose(weight.reshape(3, 9, channels, channels), (1, 0, 2, 3))
    parts = jnp.einsum("tkoc,tohw->kchw", tap_weights, slices, preferred_element_type=jnp.float32)
    term_zero = parts[0].astype(jnp.bfloat16)
    term_one = parts[1].astype(jnp.bfloat16)
    later_zero, later_one = passed_along((term_zero, term_one), "tm", -1)
    far_zero = passed_along(later_zero, "tm", -1)
    input_grad = (parts[2] + later_one.astype(jnp.float32) + far_zero.astype(jnp.float32)).astype(
        jnp.bfloat16
    )[None]
    own_terms = jnp.stack([parts[0], parts[1]], axis=0)
    second_terms = jnp.stack([jnp.zeros_like(parts[0]), term_zero.astype(jnp.float32)], axis=0)
    cache_terms = jnp.where(
        group_index == 0,
        own_terms,
        jnp.where(group_index == 1, second_terms, jnp.zeros_like(own_terms)),
    )
    cache_grad = lax.psum_scatter(cache_terms, "tm", scatter_dimension=1, tiled=True).astype(
        jnp.bfloat16
    )
    scale = 1.0 / math.sqrt(lax.axis_size("tm") * lax.axis_size("space") * row_count * col_count)

    def tap_block(row_tap, col_tap):
        shifted = input_pad[:, :, row_tap : row_tap + row_count, col_tap : col_tap + col_count]
        return jnp.einsum("ohw,kchw->koc", grad_rows, shifted, preferred_element_type=jnp.float32)

    blocks = jnp.stack(
        [
            jnp.stack([tap_block(row_tap, col_tap) for col_tap in range(3)], axis=0)
            for row_tap in range(3)
        ],
        axis=0,
    )
    summed = lax.psum(blocks, ("tm", "space"))
    weight_grad = jnp.transpose(summed, (2, 0, 1, 3, 4)) * scale
    return (input_grad, cache_grad, weight_grad)


def solution(mesh):
    placed = (
        P("tm", None, "space", None),
        P(None, "tm", "space", None),
        P("tm", None, "space", None),
        P(),
    )
    return jax.shard_map(
        per_device,
        mesh=mesh,
        in_specs=placed,
        out_specs=(P("tm", None, "space", None), P(None, "tm", "space", None), P()),
        check_vma=False,
    )
```

profile of v0, /device:TPU:0, one launch (start us, length us, event | category | flops | bytes accessed | tf_op | source)
XLA Modules:
  0.0 362.6 jit_solution(7171910444510837045)
XLA Ops:
  7.2 1.9 copy.8
  11.4 5.0 %collective-permute-start = (bf16[1,96,4,1280]{3,1,2,0:T(8,128)(2,1)S(1)}, bf16[1,96,4,1280]{3,1,2,0:T(8,128)(2,1)S(1)}, u32[]{:S(2)}, u32[]{:S(2)}) collective-permute-start(bf16[1,96,4,1280]{3,1,2,0:T(8,128)(2,1)S(1)} %copy.7), channel_id=1, source_target_pairs={{0,8},{8,16},{16,24},{1,9},{9,17},{17,25},{2,10},{10,18},{18,26},{... | collective-permute-start | bytes 2949128 | tf_op jit(solution)/shard_map/ppermute | solution.py:12
  16.4 38.3 %collective-permute-done = bf16[1,96,4,1280]{3,1,2,0:T(8,128)(2,1)S(1)} collective-permute-done((bf16[1,96,4,1280]{3,1,2,0:T(8,128)(2,1)S(1)}, bf16[1,96,4,1280]{3,1,2,0:T(8,128)(2,1)S(1)}, u32[]{:S(2)}, u32[]{:S(2)}) %collective-permute-start) | collective-permute-done | bytes 983072 | tf_op jit(solution)/shard_map/ppermute | solution.py:12
  54.7 17.7 %collective-permute-start.1 = (bf16[1,96,4,1280]{3,1,2,0:T(8,128)(2,1)S(1)}, bf16[1,96,4,1280]{3,1,2,0:T(8,128)(2,1)S(1)}, u32[]{:S(2)}, u32[]{:S(2)}) collective-permute-start(bf16[1,96,4,1280]{3,1,2,0:T(8,128)(2,1)S(1)} %collective-permute-done), channel_id=1, source_target_pairs={{0,8},{8,16},{16,24},{1,9},{9,17},{17,25},{2,10},{10,18},{18,26},{... | collective-permute-start | bytes 2949128 | tf_op jit(solution)/shard_map/ppermute | solution.py:12
  72.5 2.3 copy.10
  74.8 15.4 %collective-permute-done.1 = bf16[1,96,4,1280]{3,1,2,0:T(8,128)(2,1)S(1)} collective-permute-done((bf16[1,96,4,1280]{3,1,2,0:T(8,128)(2,1)S(1)}, bf16[1,96,4,1280]{3,1,2,0:T(8,128)(2,1)S(1)}, u32[]{:S(2)}, u32[]{:S(2)}) %collective-permute-start.1) | collective-permute-done | bytes 983072 | tf_op jit(solution)/shard_map/ppermute | solution.py:12
  91.2 1.8 fusion.92
  93.3 1.5 pad_maximum_fusion.4
  94.8 2.3 collective-permute-start.2
  99.5 2.4 fusion.54
  102.6 8.5 %select_maximum_fusion = bf16[4,96,6,1282]{3,1,2,0:T(8,128)(2,1)S(1)} fusion(bf16[4,96,1,1280]{3,1,2,0:T(8,128)(2,1)} %collective-permute-done.3, bf16[4,96,1,1280]{3,1,2,0:T(8,128)(2,1)} %collective-permute-done.2, bf16[1,96,4,1280]{3,1,2,0:T(8,128)(2,1)} %copy.10, bf16[1,96,4,1280]{3,1,2,0:T(8,128)(2,1)} %copy-done.3, ...), kind=kLoop, calls=%fused_computation.5 | loop fusion | flops 62028288 | bytes 11805696 | tf_op jit(solution)/shard_map/concatenate | solution.py:21
  112.0 1.3 fusion.66
  118.1 2.0 fusion.57
  120.2 2.0 fusion.60
  126.3 3.7 %fusion.30 = f32[3,96,4,1280]{3,1,0,2:T(8,128)S(1)} fusion(bf16[9,96,4,1280]{3,1,0,2:T(8,128)(2,1)S(1)} %fusion.83, bf16[3,9,96,96]{2,3,1,0:T(8,128)(2,1)S(1)} %copy-done.12), kind=kOutput, calls=%fused_computation.34 | convolution fusion | flops 2548039680 | bytes 15243264 | tf_op jit(solution)/shard_map/tkoc,tohw->kchw/dot_general | solution.py:61
  130.2 2.3 copy-done
  132.5 2.3 slice_select_fusion
  138.4 13.3 %collective-permute-done.5 = bf16[96,4,1280]{2,0,1:T(8,128)(2,1)} collective-permute-done((bf16[96,4,1280]{2,0,1:T(8,128)(2,1)S(1)}, bf16[96,4,1280]{2,0,1:T(8,128)(2,1)}, u32[]{:S(2)}, u32[]{:S(2)}) %collective-permute-start.5) | collective-permute-done | bytes 983072 | tf_op jit(solution)/shard_map/ppermute | solution.py:12
  153.0 125.6 %all-reduce.4.cloned.1.call-done = f32[3,3,3,96,96]{3,4,2,1,0:T(8,128)} async-done(((f32[3,3,3,96,96]{3,4,2,1,0:T(8,128)}), f32[3,3,3,96,96]{3,4,2,1,0:T(8,128)}) %all-reduce.4.cloned.1.call-update) | async-done | bytes 995344 | tf_op jit(solution)/shard_map/psum | solution.py:92
  278.6 1.4 multiply_bitcast_fusion
  280.1 1.5 copy.34
  281.6 1.8 fusion.81
  283.4 1.7 copy.32
  285.1 68.7 %reduce-scatter.2.cloned.1.call-done = f32[2,24,4,1280]{3,1,0,2:T(8,128)} async-done(((f32[2,96,4,1280]{3,1,0,2:T(8,128)}), f32[2,24,4,1280]{3,1,0,2:T(8,128)}) %reduce-scatter.2.cloned.1.call-update) | async-done | bytes 983056 | tf_op jit(solution)/shard_map/reduce_scatter | solution.py:76
  (64 shorter events, 23.6 us)
Async XLA Ops:
  7.2 84.0 %all-gather.2.cloned.1.call-start = ((), (), s32[]{:S(2)}) async-start(), calls=%async_computation.1 | async-start | bytes 2457600 | tf_op jit(solution)/shard_map/all_gather | solution.py:39
  9.1 269.5 %all-reduce.4.cloned.1.call-start = ((), (), s32[]{:S(2)}) async-start(), calls=%async_computation.3 | async-start | bytes 2654208 | tf_op jit(solution)/shard_map/psum | solution.py:92
  10.4 0.9 copy-start.3
  11.4 43.3 %collective-permute-start = (bf16[1,96,4,1280]{3,1,2,0:T(8,128)(2,1)S(1)}, bf16[1,96,4,1280]{3,1,2,0:T(8,128)(2,1)S(1)}, u32[]{:S(2)}, u32[]{:S(2)}) collective-permute-start(bf16[1,96,4,1280]{3,1,2,0:T(8,128)(2,1)S(1)} %copy.7), channel_id=1, source_target_pairs={{0,8},{8,16},{16,24},{1,9},{9,17},{17,25},{2,10},{10,18},{18,26},{... | collective-permute-start | bytes 2949128 | tf_op jit(solution)/shard_map/ppermute | solution.py:12
  54.7 35.5 %copy-start.8 = (bf16[1,96,4,1280]{3,1,2,0:T(8,128)(2,1)}, bf16[1,96,4,1280]{3,1,2,0:T(8,128)(2,1)S(1)}, u32[]{:S(2)}) copy-start(bf16[1,96,4,1280]{3,1,2,0:T(8,128)(2,1)S(1)} %collective-permute-done) | copy-start | bytes 2949124
  54.7 35.5 %collective-permute-start.1 = (bf16[1,96,4,1280]{3,1,2,0:T(8,128)(2,1)S(1)}, bf16[1,96,4,1280]{3,1,2,0:T(8,128)(2,1)S(1)}, u32[]{:S(2)}, u32[]{:S(2)}) collective-permute-start(bf16[1,96,4,1280]{3,1,2,0:T(8,128)(2,1)S(1)} %collective-permute-done), channel_id=1, source_target_pairs={{0,8},{8,16},{16,24},{1,9},{9,17},{17,25},{2,10},{10,18},{18,26},{... | collective-permute-start | bytes 2949128 | tf_op jit(solution)/shard_map/ppermute | solution.py:12
  72.5 25.8 %copy-start.11 = (bf16[3,3,3,96,96]{4,3,2,1,0:T(8,128)(2,1)S(1)}, bf16[3,3,3,96,96]{4,3,2,1,0:T(8,128)(2,1)}, u32[]{:S(2)}) copy-start(bf16[3,3,3,96,96]{4,3,2,1,0:T(8,128)(2,1)} %param.7) | copy-start | bytes 1492996
  90.2 1.0 copy-start.9
  91.2 1.9 copy-start.4
  91.2 2.1 copy-start.6
  93.0 9.6 %copy-start.1 = (bf16[1,96,4,1280]{3,1,2,0:T(8,128)(2,1)}, bf16[1,96,4,1280]{3,1,2,0:T(8,128)(2,1)S(1)}, u32[]{:S(2)}) copy-start(bf16[1,96,4,1280]{3,1,2,0:T(8,128)(2,1)S(1)} %get-tuple-element.11) | copy-start | bytes 2949124
  94.8 7.1 %collective-permute-start.2 = (bf16[4,96,1,1280]{3,1,2,0:T(8,128)(2,1)}, bf16[4,96,1,1280]{3,1,2,0:T(8,128)(2,1)}, u32[]{:S(2)}, u32[]{:S(2)}) collective-permute-start(bf16[4,96,1,1280]{3,1,2,0:T(8,128)(2,1)} %get-tuple-element.8), channel_id=1, source_target_pairs={{0,1},{1,2},{2,3},{3,4},{4,5},{5,6},{6,7},{8,9},{9,10},{10,11},{11... | collective-permute-start | bytes 2949128 | tf_op jit(solution)/shard_map/ppermute | solution.py:23
  97.1 5.6 %collective-permute-start.3 = (bf16[4,96,1,1280]{3,1,2,0:T(8,128)(2,1)}, bf16[4,96,1,1280]{3,1,2,0:T(8,128)(2,1)}, u32[]{:S(2)}, u32[]{:S(2)}) collective-permute-start(bf16[4,96,1,1280]{3,1,2,0:T(8,128)(2,1)} %get-tuple-element.9), channel_id=1, source_target_pairs={{1,0},{2,1},{3,2},{4,3},{5,4},{6,5},{7,6},{9,8},{10,9},{11,10},{12... | collective-permute-start | bytes 2949128 | tf_op jit(solution)/shard_map/ppermute | solution.py:25
  101.9 9.2 %copy-start.10 = (bf16[1,96,4,1280]{3,2,1,0:T(4,128)(2,1)S(1)}, bf16[1,96,4,1280]{3,2,1,0:T(4,128)(2,1)}, u32[]{:S(2)}) copy-start(bf16[1,96,4,1280]{3,2,1,0:T(4,128)(2,1)} %param.6) | copy-start | bytes 2949124
  115.6 2.4 copy-start.2
  115.6 2.4 copy-start.5
  115.6 2.4 copy-start.7
  123.5 230.4 %reduce-scatter.2.cloned.1.call-start = ((), (), s32[]{:S(2)}) async-start(), calls=%async_computation.2 | async-start | bytes 4915200 | tf_op jit(solution)/shard_map/reduce_scatter | solution.py:76
  124.5 1.9 copy-start.12
  130.0 2.5 copy-start
  134.8 16.9 %collective-permute-start.5 = (bf16[96,4,1280]{2,0,1:T(8,128)(2,1)S(1)}, bf16[96,4,1280]{2,0,1:T(8,128)(2,1)}, u32[]{:S(2)}, u32[]{:S(2)}) collective-permute-start(bf16[96,4,1280]{2,0,1:T(8,128)(2,1)S(1)} %bitcast.187), channel_id=1, source_target_pairs={{8,0},{16,8},{24,16},{9,1},{17,9},{25,17},{10,2},{18,10},{26,18},{... | collective-permute-start | bytes 2949128 | tf_op jit(solution)/shard_map/ppermute | solution.py:12
  137.1 144.4 %collective-permute-start.4 = (bf16[96,4,1280]{2,0,1:T(8,128)(2,1)}, bf16[96,4,1280]{2,0,1:T(8,128)(2,1)S(1)}, u32[]{:S(2)}, u32[]{:S(2)}) collective-permute-start(bf16[96,4,1280]{2,0,1:T(8,128)(2,1)} %bitcast.186), channel_id=1, source_target_pairs={{8,0},{16,8},{24,16},{9,1},{17,9},{25,17},{10,2},{18,10},{26,18},{... | collective-permute-start | bytes 2949128 | tf_op jit(solution)/shard_map/ppermute | solution.py:12
  151.7 129.9 %collective-permute-start.6 = (bf16[96,4,1280]{2,0,1:T(8,128)(2,1)}, bf16[96,4,1280]{2,0,1:T(8,128)(2,1)S(1)}, u32[]{:S(2)}, u32[]{:S(2)}) collective-permute-start(bf16[96,4,1280]{2,0,1:T(8,128)(2,1)} %collective-permute-done.5), channel_id=1, source_target_pairs={{8,0},{16,8},{24,16},{9,1},{17,9},{25,17},{10,2},{18,10},{26,18},{... | collective-permute-start | bytes 2949128 | tf_op jit(solution)/shard_map/ppermute | solution.py:12
Sparse Core Ops, SparseCore 0:
  10.1 59.8 all-gather.1
  123.6 155.0 all-reduce.3
  280.9 72.8 reduce-scatter.1
where the time goes:
time: 363 us
  waiting for transfers between devices  262 us (72%)
  starting transfers between devices  30.4 us (8%)
  other arithmetic  19.9 us (5%)
  local copies, waits for them, and re-layouts  19.2 us (5%)
  matrix products  16.9 us (5%)
  between operations  14.1 us (4%)
    psum x1, waiting for transfers between devices, per_device(): summed = lax.psum(blocks, ('tm', 'space'))  126 us
    reduce_scatter x1, waiting for transfers between devices, per_device(): lax.psum_scatter(cache_terms, 'tm', scatter_dimension=1, tiled=True)  68.7 us
    ppermute x5, waiting for transfers between devices, passed_along(): lax.ppermute(value, axis, [(source, source + steps) for source in range(i...  67 us
    ppermute x5, starting transfers between devices, passed_along(): lax.ppermute(value, axis, [(source, source + steps) for source in range(i...  26.6 us
    unnamed x41, local copies, waits for them, and re-layouts  17.7 us
    dot_general x9, matrix products, tap_block(): jnp.einsum('ohw,kchw->koc', grad_rows, shifted, preferred_element_type=jn...  13.2 us
    concatenate x1, other arithmetic, padded_2(): jnp.concatenate([lax.ppermute(tail, axis, [(i, (i + 1) % count) for i in...  8.45 us
  transfers between devices with their start and end apart: 10, of which 6 were waited for; matrix products, arithmetic and copies ran while one was open for 6% of the time, Pallas kernels for 0%

commit v1 on v0

v1 whole, which is shorter than its diff:
```python
import functools
import math

import jax
import jax.numpy as jnp
from jax import lax
from jax.experimental import pallas as pl
from jax.experimental.pallas import tpu as pltpu
from jax.sharding import PartitionSpec as P

MESH = pl.DeviceIdType.MESH
OWN, N1, N2, C1, C0 = range(5)
TO_PREV, FWD_PREV, TO_NEXT, FWD_C1, FWD_C0 = range(5)


def kernel(
    nz, ns, chunks, channels, share, scale,
    g_ref, xs_ref, wl_ref, out_ref, wg_a_ref, wg_b_ref,
    gp, sc, dacc, wtmp, acc_a, acc_b,
    sb_a, rb_a, zs_a, zb_a, gb_a, sb_b, rb_b, zs_b, zb_b, gb_b,
    z_send, z_recv, h_send, h_recv,
    rs_send, rs_recv, zz_send, zz_recv, ag_send, ag_recv,
):
    j = lax.axis_index("tm")
    s = lax.axis_index("space")
    rows, _, cols = g_ref.shape
    k_row = 3 * channels
    taps = 3 * k_row
    last = nz - 1

    barrier = pltpu.get_barrier_semaphore()
    for k in range(1, ns):
        pl.semaphore_signal(barrier, inc=1, device_id={"space": lax.rem(s + k, ns)}, device_id_type=MESH)
    for k in range(1, nz):
        pl.semaphore_signal(barrier, inc=1, device_id={"tm": lax.rem(j + k, nz)}, device_id_type=MESH)
    pl.semaphore_wait(barrier, ns - 1 + nz - 1)

    def row_copy(stream, slot_from, slot_to, r, target):
        src = g_ref.at[r] if slot_from == OWN else gp.at[slot_from, r + 1]
        return pltpu.make_async_remote_copy(
            src_ref=src, dst_ref=gp.at[slot_to, r + 1],
            send_sem=z_send.at[stream, r], recv_sem=z_recv.at[slot_to, r],
            device_id={"tm": target}, device_id_type=MESH)

    prev = lax.rem(j + nz - 1, nz)
    nxt = lax.rem(j + 1, nz)

    def to_prev(r):
        return row_copy(TO_PREV, OWN, N1, r, prev)

    def fwd_prev(r):
        return row_copy(FWD_PREV, N1, N2, r, prev)

    def own_c0(r):
        return row_copy(TO_NEXT, OWN, C0, r, nxt)

    def own_c1(r):
        return row_copy(TO_NEXT, OWN, C1, r, nxt)

    def fwd_c1(r):
        return row_copy(FWD_C1, C1, C1, r, nxt)

    def fwd_c0(r):
        return row_copy(FWD_C0, C0, C0, r, nxt)

    for r in range(rows):
        pl.when(j >= 1)(lambda: to_prev(r).start())
        pl.when(j == 0)(lambda: own_c0(r).start())
        if nz > 2:
            pl.when(j == 1)(lambda: own_c1(r).start())

    def halo_up(slot):
        src = g_ref.at[0] if slot == OWN else gp.at[slot, 1]
        return pltpu.make_async_remote_copy(
            src_ref=src, dst_ref=gp.at[slot, rows + 1],
            send_sem=h_send.at[slot, 0], recv_sem=h_recv.at[slot, 0],
            device_id={"space": lax.rem(s + ns - 1, ns)}, device_id_type=MESH)

    def halo_down(slot):
        src = g_ref.at[rows - 1] if slot == OWN else gp.at[slot, rows]
        return pltpu.make_async_remote_copy(
            src_ref=src, dst_ref=gp.at[slot, 0],
            send_sem=h_send.at[slot, 1], recv_sem=h_recv.at[slot, 1],
            device_id={"space": lax.rem(s + 1, ns)}, device_id_type=MESH)

    def halo_start_up(slot):
        pl.when(s >= 1)(lambda: halo_up(slot).start())

    def halo_start_down(slot):
        pl.when(s < ns - 1)(lambda: halo_down(slot).start())

    def halo_wait(slot):
        @pl.when(s >= 1)
        def _():
            halo_up(slot).wait_send()
            halo_down(slot).wait_recv()

        @pl.when(s < ns - 1)
        def _():
            halo_down(slot).wait_send()
            halo_up(slot).wait_recv()

    halo_start_up(OWN)
    halo_start_down(OWN)

    @pl.when(s == 0)
    def _():
        for slot in range(5):
            gp[slot, 0] = jnp.zeros(gp.shape[2:], gp.dtype)

    @pl.when(s == ns - 1)
    def _():
        for slot in range(5):
            gp[slot, rows + 1] = jnp.zeros(gp.shape[2:], gp.dtype)

    dacc[...] = jnp.zeros_like(dacc)
    acc_a[...] = jnp.zeros_like(acc_a)
    acc_b[...] = jnp.zeros_like(acc_b)
    wtmp[...] = jnp.zeros_like(wtmp)
    for r in range(rows):
        gp[OWN, r + 1] = g_ref[r]

    lane = lax.broadcasted_iota(jnp.int32, (channels, cols), 1)
    tile = 256 if cols % 256 == 0 else 128
    tiles = cols // tile
    stack = xs_ref.shape[1]
    wide = 128
    wlane = lax.broadcasted_iota(jnp.int32, (taps, wide), 1)

    def shift_row(slot, p):
        value = gp[slot, p]
        full = value.astype(jnp.float32)
        ahead = jnp.where(lane == cols - 1, 0.0, pltpu.roll(full, cols - 1, 1))
        behind = jnp.where(lane == 0, 0.0, pltpu.roll(full, 1, 1))
        base = pl.multiple_of(p * k_row, 16)
        sc[pl.ds(base, channels), :] = ahead.astype(jnp.bfloat16)
        sc[pl.ds(pl.multiple_of(base + channels, 16), channels), :] = value
        sc[pl.ds(pl.multiple_of(base + 2 * channels, 16), channels), :] = behind.astype(jnp.bfloat16)

    def compute_row(slot, h, first):
        base = pl.multiple_of(h * k_row, 16)

        def col_step(i, carry):
            at = pl.multiple_of(i * tile, tile)
            block = sc[pl.ds(base, taps), pl.ds(at, tile)]
            dacc[h, :, pl.ds(at, tile)] += jnp.dot(
                wl_ref[slot], block, preferred_element_type=jnp.float32)
            part = lax.dot_general(
                block, xs_ref[h, :, pl.ds(at, tile)], (((1,), (1,)), ((), ())),
                preferred_element_type=jnp.float32)
            wtmp[:, :stack] += part
            return carry

        lax.fori_loop(0, tiles, col_step, 0)

    def placed_cache(block, shift_from):
        turned = pltpu.roll(block, lax.rem(j * share + 2 * wide - shift_from, wide), 1)
        inside = jnp.logical_and(wlane >= j * share, wlane < (j + 1) * share)
        return jnp.where(inside, turned, 0.0)

    def process(slot, hook=None):
        def do_shift(p, carry):
            shift_row(slot, p)
            return carry

        lax.fori_loop(0, rows + 2, do_shift, 0)
        if hook is None:
            def do_row(h, carry):
                compute_row(slot, h, False)
                return carry

            lax.fori_loop(0, rows, do_row, 0)
        else:
            for h in range(rows):
                hook(h)
                compute_row(slot, h, False)
        low = wtmp[:, :wide]
        x_part = jnp.where(wlane < channels, low, 0.0)
        if slot == OWN:
            acc_a[:taps, :] += x_part
        if slot == N1:
            acc_b[:taps, :] += x_part
        if slot == N2:
            acc_b[taps:2 * taps, :] += x_part

        def as_g0():
            acc_b[taps:2 * taps, :] += placed_cache(wtmp[:, :wide], channels)
            acc_b[:taps, :] += placed_cache(wtmp[:, wide:], 0)

        def as_g1():
            acc_b[taps:2 * taps, :] += placed_cache(wtmp[:, wide:], 0)

        if slot == OWN:
            pl.when(j == 0)(as_g0)
            pl.when(j == 1)(as_g1)
        if slot == N1:
            pl.when(j == 0)(as_g1)
        if slot == C1:
            as_g1()
        if slot == C0:
            as_g0()
        wtmp[...] = jnp.zeros_like(wtmp)

    def reduction(index, acc, sb, rb, zs, zb, gb, out, ck):
        def rs_copy(k):
            to = lax.rem(s + k, ns)
            return pltpu.make_async_remote_copy(
                src_ref=sb.at[to], dst_ref=rb.at[s],
                send_sem=rs_send.at[index, k], recv_sem=rs_recv.at[index, s],
                device_id={"space": to}, device_id_type=MESH)

        def rs_landed(k):
            source = lax.rem(s + ns - k, ns)
            return pltpu.make_async_remote_copy(
                src_ref=sb.at[source], dst_ref=rb.at[source],
                send_sem=rs_send.at[index, k], recv_sem=rs_recv.at[index, source],
                device_id={"space": source}, device_id_type=MESH)

        def z_copy(k):
            return pltpu.make_async_remote_copy(
                src_ref=zs, dst_ref=zb.at[j],
                send_sem=zz_send.at[index, k], recv_sem=zz_recv.at[index, j],
                device_id={"tm": lax.rem(j + k, nz)}, device_id_type=MESH)

        def z_landed(k):
            source = lax.rem(j + nz - k, nz)
            return pltpu.make_async_remote_copy(
                src_ref=zs, dst_ref=zb.at[source],
                send_sem=zz_send.at[index, k], recv_sem=zz_recv.at[index, source],
                device_id={"tm": source}, device_id_type=MESH)

        def ag_copy(k):
            return pltpu.make_async_remote_copy(
                src_ref=gb.at[s], dst_ref=gb.at[s],
                send_sem=ag_send.at[index, k], recv_sem=ag_recv.at[index, s],
                device_id={"space": lax.rem(s + k, ns)}, device_id_type=MESH)

        def ag_landed(k):
            source = lax.rem(s + ns - k, ns)
            return pltpu.make_async_remote_copy(
                src_ref=gb.at[source], dst_ref=gb.at[source],
                send_sem=ag_send.at[index, k], recv_sem=ag_recv.at[index, source],
                device_id={"space": source}, device_id_type=MESH)

        def scatter():
            for q in range(ns):
                sb[q] = acc[q * ck:(q + 1) * ck, :].astype(jnp.bfloat16)
            for k in range(1, ns):
                rs_copy(k).start()

        def across():
            total = acc[pl.ds(pl.multiple_of(s * ck, 16), ck), :]
            for k in range(1, ns):
                rs_landed(k).wait_recv()
                total = total + rb[lax.rem(s + ns - k, ns)].astype(jnp.float32)
            zs[...] = total
            for k in range(1, nz):
                z_copy(k).start()

        def gather():
            zb[j] = zs[...]
            for k in range(1, nz):
                z_landed(k).wait_recv()
            total = zb[0]
            for q in range(1, nz):
                total = total + zb[q]
            gb[s] = (total * scale).astype(jnp.bfloat16)
            for k in range(1, ns):
                ag_copy(k).start()

        def finish():
            for k in range(1, ns):
                ag_landed(k).wait_recv()
            for q in range(ns):
                out[q * ck:(q + 1) * ck, :] = gb[q].astype(jnp.float32)
            for k in range(1, ns):
                rs_copy(k).wait_send()
                ag_copy(k).wait_send()
            for k in range(1, nz):
                z_copy(k).wait_send()

        return scatter, across, gather, finish

    a_steps = reduction(0, acc_a, sb_a, rb_a, zs_a, zb_a, gb_a, wg_a_ref, chunks[0])
    b_steps = reduction(1, acc_b, sb_b, rb_b, zs_b, zb_b, gb_b, wg_b_ref, chunks[1])

    halo_wait(OWN)
    process(OWN)
    a_steps[0]()

    has_n1 = j < last
    has_n2 = j < last - 1
    for r in range(rows):
        @pl.when(has_n1)
        def _():
            to_prev(r).wait_recv()
            pl.when(j >= 1)(lambda: fwd_prev(r).start())
            if r == 0:
                halo_start_up(N1)
            if r == rows - 1:
                halo_start_down(N1)

        @pl.when(j == 1)
        def _():
            own_c0(r).wait_recv()
            if nz > 2:
                fwd_c0(r).start()
            if r == 0:
                halo_start_up(C0)
            if r == rows - 1:
                halo_start_down(C0)

        if nz > 2:
            @pl.when(j >= 2)
            def _():
                own_c1(r).wait_recv()
                pl.when(j < last)(lambda: fwd_c1(r).start())
                if r == 0:
                    halo_start_up(C1)
                if r == rows - 1:
                    halo_start_down(C1)

    @pl.when(has_n1)
    def _():
        halo_wait(N1)
        process(N1)

    a_steps[1]()

    def c0_row(r):
        own_c0(r).wait_recv()
        pl.when(j < last)(lambda: fwd_c0(r).start())
        if r == 0:
            halo_start_up(C0)
        if r == rows - 1:
            halo_start_down(C0)

    if nz > 2:
        @pl.when(j >= 2)
        def _():
            halo_wait(C1)
            process(C1, c0_row)

    @pl.when(j >= 1)
    def _():
        halo_wait(C0)
        process(C0)

    a_steps[2]()

    if nz > 2:
        @pl.when(has_n2)
        def _():
            for r in range(rows):
                fwd_prev(r).wait_recv()
                if r == 0:
                    halo_start_up(N2)
                if r == rows - 1:
                    halo_start_down(N2)
            halo_wait(N2)
            process(N2)

    b_steps[0]()
    out_ref[...] = dacc[...].astype(jnp.bfloat16)
    a_steps[3]()
    b_steps[1]()
    b_steps[2]()

    for r in range(rows):
        @pl.when(j >= 1)
        def _():
            to_prev(r).wait_send()

        @pl.when(jnp.logical_and(j >= 1, has_n1))
        def _():
            fwd_prev(r).wait_send()

        @pl.when(j == 0)
        def _():
            own_c0(r).wait_send()

        if nz > 2:
            @pl.when(j == 1)
            def _():
                own_c1(r).wait_send()

            @pl.when(jnp.logical_and(j >= 1, j < last))
            def _():
                fwd_c0(r).wait_send()

            @pl.when(jnp.logical_and(j >= 2, j < last))
            def _():
                fwd_c1(r).wait_send()
    b_steps[3]()


def up_to(value, step):
    return -(-value // step) * step


def per_device(nz, ns, frames, cache, grad_out, weight):
    j = lax.axis_index("tm")
    _, channels, rows, cols = frames.shape
    share = cache.shape[1]
    taps = 9 * channels
    gap = up_to(share, 32) - share
    lead = 128 - channels
    stack = 128 + up_to(share, 32)
    g = jnp.transpose(grad_out[0], (1, 0, 2))

    def stacked(x_rows, first, second, dim):
        def empty(like, count):
            shape = list(like.shape)
            shape[dim] = count
            return jnp.zeros(shape, like.dtype)

        parts = [x_rows, first]
        if lead > share:
            parts.append(empty(first, lead - share))
        parts.append(second)
        if gap:
            parts.append(empty(second, gap))
        return jnp.concatenate(parts, axis=dim)

    xs = stacked(
        jnp.transpose(frames[0], (1, 0, 2)), jnp.transpose(cache[0], (1, 0, 2)),
        jnp.transpose(cache[1], (1, 0, 2)), 1)
    wt = jnp.transpose(weight[:, ::-1], (0, 4, 1, 2, 3)).reshape(3, channels, taps)
    wc = lax.dynamic_slice_in_dim(wt, j * share, share, axis=1)
    zx = jnp.zeros_like(wt[0])
    zc = jnp.zeros_like(wc[0])

    def pick(is_g0, is_g1):
        first = jnp.where(is_g0, wc[0], zc)
        second = jnp.where(is_g0, wc[1], jnp.where(is_g1, wc[0], zc))
        return first, second

    no = jnp.zeros((), bool)
    wl = jnp.stack([
        stacked(wt[2], *pick(j == 0, j == 1), 0),
        stacked(wt[1], *pick(no, j == 0), 0),
        stacked(wt[0], zc, zc, 0),
        stacked(zx, zc, wc[0], 0),
        stacked(zx, wc[0], wc[1], 0),
    ])
    chunks = (up_to(-(-taps // ns), 16), up_to(-(-2 * taps // ns), 16))
    scale = 1.0 / math.sqrt(nz * ns * rows * cols)
    f32, bf16 = jnp.float32, jnp.bfloat16

    def buffers(ck):
        return [
            pltpu.VMEM((ns, ck, 128), bf16), pltpu.VMEM((ns, ck, 128), bf16),
            pltpu.VMEM((ck, 128), f32), pltpu.VMEM((nz, ck, 128), f32),
            pltpu.VMEM((ns, ck, 128), bf16)]

    vmem = pl.BlockSpec(memory_space=pltpu.VMEM)
    dma = pltpu.SemaphoreType.DMA
    out, wg_a, wg_b = pl.pallas_call(
        functools.partial(kernel, nz, ns, chunks, channels, share, scale),
        out_shape=(
            jax.ShapeDtypeStruct((rows, stack, cols), bf16),
            jax.ShapeDtypeStruct((ns * chunks[0], 128), f32),
            jax.ShapeDtypeStruct((ns * chunks[1], 128), f32),
        ),
        in_specs=[vmem] * 3,
        out_specs=(vmem,) * 3,
        scratch_shapes=[
            pltpu.VMEM((5, rows + 2, channels, cols), bf16),
            pltpu.VMEM(((rows + 2) * 3 * channels, cols), bf16),
            pltpu.VMEM((rows, stack, cols), f32),
            pltpu.VMEM((taps, 256), f32),
            pltpu.VMEM((ns * chunks[0], 128), f32),
            pltpu.VMEM((ns * chunks[1], 128), f32),
            *buffers(chunks[0]), *buffers(chunks[1]),
            dma((5, rows)), dma((5, rows)), dma((5, 2)), dma((5, 2)),
            dma((2, ns)), dma((2, ns)), dma((2, nz)), dma((2, nz)), dma((2, ns)), dma((2, ns)),
        ],
        compiler_params=pltpu.CompilerParams(
            collective_id=0, has_side_effects=True, vmem_limit_bytes=60 * 1024 * 1024),
    )(g, xs, wl)
    input_grad = jnp.transpose(out[:, :channels], (1, 0, 2))[None]
    cache_grad = jnp.stack([
        jnp.transpose(out[:, channels:channels + share], (1, 0, 2)),
        jnp.transpose(out[:, 128:128 + share], (1, 0, 2))])

    def unpacked(rows_of, count):
        cut = rows_of[:count * taps, :channels].reshape(count, 3, 3, channels, channels)
        return cut[:, ::-1]

    low = unpacked(wg_b, 2)
    weight_grad = jnp.concatenate([low[1:], low[:1], unpacked(wg_a, 1)], axis=0)
    return (input_grad, cache_grad, weight_grad)


def solution(mesh):
    placed = (
        P("tm", None, "space", None),
        P(None, "tm", "space", None),
        P("tm", None, "space", None),
        P(),
    )
    return jax.shard_map(
        functools.partial(per_device, mesh.shape["tm"], mesh.shape["space"]),
        mesh=mesh,
        in_specs=placed,
        out_specs=(P("tm", None, "space", None), P(None, "tm", "space", None), P()),
        check_vma=False,
    )
```

time: 363 us -> 128 us (0.35)
  waiting for transfers between devices: 262 us -> 0 us
  Pallas kernels: 0 us -> 105 us
  starting transfers between devices: 30.4 us -> 0 us
  other arithmetic: 19.9 us -> 2.48 us
  matrix products: 16.9 us -> 0 us
  between operations: 14.1 us -> 0.93 us
    psum x1 -> x0, waiting for transfers between devices: 126 us -> none  [per_device(): summed = lax.psum(blocks, ('tm', 'space'))]
    pallas_call x0 -> x1, Pallas kernels: none -> 105 us  [per_device(): pl.pallas_call(functools.partial(kernel, nz, ns, chunks, channels, share,...]
    reduce_scatter x1 -> x0, waiting for transfers between devices: 68.7 us -> none  [per_device(): lax.psum_scatter(cache_terms, 'tm', scatter_dimension=1, tiled=True)]
    ppermute x7 -> x0, waiting for transfers between devices: 67.7 us -> none  [the longest x5 67 us: passed_along(): lax.ppermute(value, axis, [(source, source + steps) for source in range(i...]
    ppermute x7 -> x0, starting transfers between devices: 30.1 us -> none  [the longest x5 26.6 us: passed_along(): lax.ppermute(value, axis, [(source, source + steps) for source in range(i...]
    dot_general x10 -> x0, matrix products: 16.9 us -> none  [the longest x9 13.2 us: tap_block(): jnp.einsum('ohw,kchw->koc', grad_rows, shifted, preferred_element_type=jn...]
    concatenate x1, other arithmetic: 8.45 us -> 1.16 us  [per_device(): weight_grad = jnp.concatenate([low[1:], low[:1], unpacked(wg_a, 1)], axis=0)]
    unnamed x41 -> x45, local copies, waits for them, and re-layouts: 17.7 us -> 12.2 us
  transfers between devices with their start and end apart: 10 -> 0, of which waited for: 6 -> 0; matrix products, arithmetic and copies ran while one was open for 6% -> 0% of each run, Pallas kernels for 0% -> 0%
where the time goes in v1:
time: 128 us; the launch traced here: 126 us
  Pallas kernels  105 us (82%)
  local copies, waits for them, and re-layouts  17.6 us (14%)
  other arithmetic  2.48 us (2%)
    pallas_call x1, Pallas kernels, per_device(): pl.pallas_call(functools.partial(kernel, nz, ns, chunks, channels, share,...  105 us
    unnamed x45, local copies, waits for them, and re-layouts  12.2 us

profile of v1, /device:TPU:0, one launch (start us, length us, event | category | flops | bytes accessed | tf_op | source)
XLA Modules:
  0.0 125.9 jit_solution(6519478008822139739)
XLA Ops:
  0.7 0.7 broadcast_dynamic-update-slice_fusion
  1.4 1.2 fusion.4
  2.9 0.2 copy.23
  3.1 0.7 constant_dynamic-update-slice_fusion.16
  3.8 0.6 constant_dynamic-update-slice_fusion.15
  4.4 0.6 constant_dynamic-update-slice_fusion.14
  5.0 0.6 constant_dynamic-update-slice_fusion.13
  5.7 0.6 constant_dynamic-update-slice_fusion.12
  6.5 0.2 constant_dynamic-slice_fusion.1
  7.0 0.6 constant_dynamic-update-slice_fusion.24
  7.6 0.6 constant_dynamic-update-slice_fusion.4
  8.2 0.6 constant_dynamic-update-slice_fusion.22
  8.8 0.6 constant_dynamic-update-slice_fusion.21
  9.4 0.6 constant_dynamic-update-slice_fusion.17
  10.1 1.0 copy.40
  11.2 1.1 bitcast_dynamic-update-slice_fusion.3
  12.7 0.9 copy-done.2
  13.6 1.2 copy-done
  14.8 105.0 %shard_map.67 = (bf16[4,160,1280]{2,1,0:T(8,128)(2,1)}, f32[896,128]{1,0:T(8,128)}, f32[1792,128]{1,0:T(8,128)}) custom-call(bf16[4,96,1280]{2,1,0:T(8,128)(2,1)} %bitcast.69, bf16[4,160,1280]{2,1,0:T(8,128)(2,1)} %copy-done, bf16[5,160,864]{2,1,0:T(8,128)(2,1)} %copy-done.2), custom_call_target="tpu_custom_call" | custom-call | tf_op jit(solution)/shard_map/pallas_call | solution.py:458
  119.8 1.3 %fusion.2 = (f32[864,96]{1,0:T(8,128)S(1)}, f32[864,96]{1,0:T(8,128)S(1)}) fusion(f32[1792,128]{1,0:T(8,128)} %get-tuple-element.7), kind=kLoop, calls=%fused_computation.49 | loop fusion | bytes 1327104 | tf_op jit(solution)/shard_map/slice | solution.py:491
  121.2 1.2 pad_maximum_fusion
  122.4 0.7 copy-done.3
  123.2 1.7 %copy.25 = bf16[1,96,4,1280]{3,2,1,0:T(4,128)(2,1)} copy(bf16[1,96,4,1280]{3,1,2,0:T(8,128)(2,1)S(1)} %slice_bitcast_fusion) | data formatting | bytes 1966080
  125.0 1.0 copy.26
  (48 shorter events, 1.5 us)
Async XLA Ops:
  0.6 2.0 %copy-start.1 = (bf16[3,3,3,96,96]{4,3,2,1,0:T(8,128)(2,1)S(1)}, bf16[3,3,3,96,96]{4,3,2,1,0:T(8,128)(2,1)}, u32[]{:S(2)}) copy-start(bf16[3,3,3,96,96]{4,3,2,1,0:T(8,128)(2,1)} %param.7) | copy-start | bytes 1492996
  3.1 3.3 %copy-start.7 = (bf16[160,864]{1,0:T(8,128)(2,1)}, bf16[160,864]{1,0:T(8,128)(2,1)S(1)}, u32[]{:S(2)}) copy-start(bf16[160,864]{1,0:T(8,128)(2,1)S(1)} %get-tuple-element.35) | copy-start | bytes 829444
  6.4 3.6 %copy-start.4 = (bf16[1,96,4,1280]{3,2,1,0:T(4,128)(2,1)S(1)}, bf16[1,96,4,1280]{3,2,1,0:T(4,128)(2,1)}, u32[]{:S(2)}) copy-start(bf16[1,96,4,1280]{3,2,1,0:T(4,128)(2,1)} %param.6) | copy-start | bytes 2949124
  10.1 2.2 %copy-start.8 = (bf16[160,864]{1,0:T(8,128)(2,1)S(1)}, bf16[160,864]{1,0:T(8,128)(2,1)}, u32[]{:S(2)}) copy-start(bf16[160,864]{1,0:T(8,128)(2,1)} %constant_dynamic-update-slice_fusion.17) | copy-start | bytes 829444
  11.1 1.2 copy-start.6
  11.1 1.4 %copy-start.5 = (bf16[1,96,4,1280]{3,2,1,0:T(4,128)(2,1)S(1)}, bf16[1,96,4,1280]{3,2,1,0:T(4,128)(2,1)}, u32[]{:S(2)}) copy-start(bf16[1,96,4,1280]{3,2,1,0:T(4,128)(2,1)} %param.4) | copy-start | bytes 2949124
  12.5 1.1 copy-start.2
  13.6 1.2 copy-start
  119.8 1.4 %copy-start.9 = (f32[896,128]{1,0:T(8,128)S(1)}, f32[896,128]{1,0:T(8,128)}, u32[]{:S(2)}) copy-start(f32[896,128]{1,0:T(8,128)} %get-tuple-element.8) | copy-start | bytes 1376260
  121.2 1.9 %copy-start.3 = (bf16[4,160,1280]{2,1,0:T(8,128)(2,1)S(1)}, bf16[4,160,1280]{2,1,0:T(8,128)(2,1)}, u32[]{:S(2)}) copy-start(bf16[4,160,1280]{2,1,0:T(8,128)(2,1)} %get-tuple-element.6) | copy-start | bytes 4915204

commit v2 on v1

v2 whole, which is shorter than its diff:
```python
import functools
import math

import jax
import jax.numpy as jnp
from jax import lax
from jax.experimental import pallas as pl
from jax.experimental.pallas import tpu as pltpu
from jax.sharding import PartitionSpec as P

MESH = pl.DeviceIdType.MESH
OWN, N1, N2, C1, C0 = range(5)
TO_PREV, FWD_PREV, TO_NEXT, FWD_C1, FWD_C0 = range(5)


def kernel(
    nz, ns, ck, channels, share, scale,
    g_ref, x_ref, c_ref, wt_ref, wc_ref, ig_ref, cg_ref, wg_ref,
    gp, sc, dacc, wtmp, acc, xs_ref, wl_ref,
    sb, rb, zs, zb, gb,
    z_send, z_recv, h_send, h_recv,
    rs_send, rs_recv, zz_send, zz_recv, ag_send, ag_recv,
):
    assert nz == 4
    j = lax.axis_index("tm")
    s = lax.axis_index("space")
    rows, _, cols = g_ref.shape
    k_row = 3 * channels
    taps = 3 * k_row
    last = nz - 1
    order = [0, rows - 1, *range(1, rows - 1)]
    high = 128
    late = jnp.where(j < last - 1, N2, C1)

    barrier = pltpu.get_barrier_semaphore()
    for k in range(1, ns):
        pl.semaphore_signal(barrier, inc=1, device_id={"space": lax.rem(s + k, ns)}, device_id_type=MESH)
    for k in range(1, nz):
        pl.semaphore_signal(barrier, inc=1, device_id={"tm": lax.rem(j + k, nz)}, device_id_type=MESH)
    pl.semaphore_wait(barrier, ns - 1 + nz - 1)

    def row_copy(stream, slot_from, slot_to, r, target):
        src = g_ref.at[r] if slot_from == OWN else gp.at[slot_from, r + 1]
        return pltpu.make_async_remote_copy(
            src_ref=src, dst_ref=gp.at[slot_to, r + 1],
            send_sem=z_send.at[stream, r], recv_sem=z_recv.at[slot_to, r],
            device_id={"tm": target}, device_id_type=MESH)

    prev = lax.rem(j + nz - 1, nz)
    nxt = lax.rem(j + 1, nz)

    def to_prev(r):
        return row_copy(TO_PREV, OWN, N1, r, prev)

    def fwd_prev(r):
        return row_copy(FWD_PREV, N1, N2, r, prev)

    def own_c0(r):
        return row_copy(TO_NEXT, OWN, C0, r, nxt)

    def own_c1(r):
        return row_copy(TO_NEXT, OWN, C1, r, nxt)

    def fwd_c1(r):
        return row_copy(FWD_C1, C1, C1, r, nxt)

    def fwd_c0(r):
        return row_copy(FWD_C0, C0, C0, r, nxt)

    for r in order:
        pl.when(j >= 1)(lambda: to_prev(r).start())
        pl.when(j == 0)(lambda: own_c0(r).start())
    pl.when(j == 1)(lambda: own_c1(order[0]).start())

    def halo_up(slot):
        src = g_ref.at[0] if slot is OWN else gp.at[slot, 1]
        return pltpu.make_async_remote_copy(
            src_ref=src, dst_ref=gp.at[slot, rows + 1],
            send_sem=h_send.at[slot, 0], recv_sem=h_recv.at[slot, 0],
            device_id={"space": lax.rem(s + ns - 1, ns)}, device_id_type=MESH)

    def halo_down(slot):
        src = g_ref.at[rows - 1] if slot is OWN else gp.at[slot, rows]
        return pltpu.make_async_remote_copy(
            src_ref=src, dst_ref=gp.at[slot, 0],
            send_sem=h_send.at[slot, 1], recv_sem=h_recv.at[slot, 1],
            device_id={"space": lax.rem(s + 1, ns)}, device_id_type=MESH)

    def halo_start_up(slot):
        pl.when(s >= 1)(lambda: halo_up(slot).start())

    def halo_start_down(slot):
        pl.when(s < ns - 1)(lambda: halo_down(slot).start())

    def halo_wait(slot):
        @pl.when(s >= 1)
        def _():
            halo_up(slot).wait_send()
            halo_down(slot).wait_recv()

        @pl.when(s < ns - 1)
        def _():
            halo_down(slot).wait_send()
            halo_up(slot).wait_recv()

    halo_start_up(OWN)
    halo_start_down(OWN)

    @pl.when(s == 0)
    def _():
        for slot in range(5):
            gp[slot, 0] = jnp.zeros(gp.shape[2:], gp.dtype)

    @pl.when(s == ns - 1)
    def _():
        for slot in range(5):
            gp[slot, rows + 1] = jnp.zeros(gp.shape[2:], gp.dtype)

    for r in range(rows):
        gp[OWN, r + 1] = g_ref[r]
    wtmp[...] = jnp.zeros_like(wtmp)
    acc[...] = jnp.zeros_like(acc)
    stack = xs_ref.shape[1]
    xs_ref[:, channels:, :] = jnp.zeros((rows, stack - channels, cols), xs_ref.dtype)
    wl_ref[:, channels:, :] = jnp.zeros((5, stack - channels, taps), wl_ref.dtype)
    for h in range(rows):
        xs_ref[h, :channels, :] = x_ref[h]
        xs_ref[h, channels:channels + share, :] = c_ref[0, h]
        xs_ref[h, high:high + share, :] = c_ref[1, h]
    for slot, tap in ((OWN, 2), (N1, 1), (N2, 0)):
        wl_ref[slot, :channels, :] = wt_ref[tap]
    for slot in (C1, C0):
        wl_ref[slot, :channels, :] = jnp.zeros((channels, taps), wl_ref.dtype)

    def weights_g0(slot):
        wl_ref[slot, channels:channels + share, :] = wc_ref[0]
        wl_ref[slot, high:high + share, :] = wc_ref[1]

    def weights_g1(slot):
        wl_ref[slot, high:high + share, :] = wc_ref[0]

    @pl.when(j == 0)
    def _():
        weights_g0(OWN)
        weights_g1(N1)

    pl.when(j == 1)(lambda: weights_g1(OWN))
    weights_g1(C1)
    weights_g0(C0)

    lane = lax.broadcasted_iota(jnp.int32, (channels, cols), 1)
    wide = 128
    wlane = lax.broadcasted_iota(jnp.int32, (taps, wide), 1)

    def shift_row(slot, p):
        value = gp[slot, p]
        full = value.astype(jnp.float32)
        ahead = jnp.where(lane == cols - 1, 0.0, pltpu.roll(full, cols - 1, 1))
        behind = jnp.where(lane == 0, 0.0, pltpu.roll(full, 1, 1))
        base = pl.multiple_of(p * k_row, 16)
        sc[pl.ds(base, channels), :] = ahead.astype(jnp.bfloat16)
        sc[pl.ds(pl.multiple_of(base + channels, 16), channels), :] = value
        sc[pl.ds(pl.multiple_of(base + 2 * channels, 16), channels), :] = behind.astype(jnp.bfloat16)

    def compute_row(slot, h):
        block = sc[pl.ds(pl.multiple_of(h * k_row, 16), taps), :]
        term = jnp.dot(wl_ref[slot], block, preferred_element_type=jnp.float32)
        if slot is OWN:
            dacc[h] = term
        else:
            dacc[h] += term
        wtmp[:, :stack] += lax.dot_general(
            block, xs_ref[h], (((1,), (1,)), ((), ())), preferred_element_type=jnp.float32)

    def placed_cache(block, shift_from):
        turned = pltpu.roll(block, lax.rem(j * share + 2 * wide - shift_from, wide), 1)
        inside = jnp.logical_and(wlane >= j * share, wlane < (j + 1) * share)
        return jnp.where(inside, turned, 0.0)

    def run(step, start, stop):
        def body(i, carry):
            step(i)
            return carry

        lax.fori_loop(start, stop, body, 0)

    def process(slot):
        run(functools.partial(shift_row, slot), 0, rows + 2)
        run(functools.partial(compute_row, slot), 0, rows)

    def add_x(tap):
        acc[tap, :taps, :] += jnp.where(wlane < channels, wtmp[:, :wide], 0.0)

    def add_g0():
        acc[0, :taps, :] += placed_cache(wtmp[:, :wide], channels)
        acc[1, :taps, :] += placed_cache(wtmp[:, wide:], 0)

    def add_g1():
        acc[0, :taps, :] += placed_cache(wtmp[:, wide:], 0)

    def clear():
        wtmp[...] = jnp.zeros_like(wtmp)

    def reduction(index):
        def rs_copy(k):
            to = lax.rem(s + k, ns)
            return pltpu.make_async_remote_copy(
                src_ref=sb.at[index, to], dst_ref=rb.at[index, s],
                send_sem=rs_send.at[index, k], recv_sem=rs_recv.at[index, s],
                device_id={"space": to}, device_id_type=MESH)

        def rs_landed(k):
            source = lax.rem(s + ns - k, ns)
            return pltpu.make_async_remote_copy(
                src_ref=sb.at[index, source], dst_ref=rb.at[index, source],
                send_sem=rs_send.at[index, k], recv_sem=rs_recv.at[index, source],
                device_id={"space": source}, device_id_type=MESH)

        def z_copy(k):
            return pltpu.make_async_remote_copy(
                src_ref=zs.at[index], dst_ref=zb.at[index, j],
                send_sem=zz_send.at[index, k], recv_sem=zz_recv.at[index, j],
                device_id={"tm": lax.rem(j + k, nz)}, device_id_type=MESH)

        def z_landed(k):
            source = lax.rem(j + nz - k, nz)
            return pltpu.make_async_remote_copy(
                src_ref=zs.at[index], dst_ref=zb.at[index, source],
                send_sem=zz_send.at[index, k], recv_sem=zz_recv.at[index, source],
                device_id={"tm": source}, device_id_type=MESH)

        def ag_copy(k):
            return pltpu.make_async_remote_copy(
                src_ref=gb.at[index, s], dst_ref=gb.at[index, s],
                send_sem=ag_send.at[index, k], recv_sem=ag_recv.at[index, s],
                device_id={"space": lax.rem(s + k, ns)}, device_id_type=MESH)

        def ag_landed(k):
            source = lax.rem(s + ns - k, ns)
            return pltpu.make_async_remote_copy(
                src_ref=gb.at[index, source], dst_ref=gb.at[index, source],
                send_sem=ag_send.at[index, k], recv_sem=ag_recv.at[index, source],
                device_id={"space": source}, device_id_type=MESH)

        def scatter():
            for q in range(ns):
                sb[index, q] = acc[index, q * ck:(q + 1) * ck, :].astype(jnp.bfloat16)
            for k in range(1, ns):
                rs_copy(k).start()

        def across():
            total = acc[index, pl.ds(pl.multiple_of(s * ck, 16), ck), :]
            for k in range(1, ns):
                rs_landed(k).wait_recv()
                total = total + rb[index, lax.rem(s + ns - k, ns)].astype(jnp.float32)
            zs[index] = total.astype(jnp.bfloat16)
            for k in range(1, nz):
                z_copy(k).start()

        def gather():
            zb[index, j] = zs[index]
            for k in range(1, nz):
                z_landed(k).wait_recv()
            total = zb[index, 0].astype(jnp.float32)
            for q in range(1, nz):
                total = total + zb[index, q].astype(jnp.float32)
            gb[index, s] = (total * scale).astype(jnp.bfloat16)
            for k in range(1, ns):
                ag_copy(k).start()

        def finish():
            for k in range(1, ns):
                ag_landed(k).wait_recv()
            for q in range(ns):
                acc[index, q * ck:(q + 1) * ck, :] = gb[index, q].astype(jnp.float32)
            for b in range(3):
                for d in range(3):
                    at = (b * 3 + d) * channels
                    wg_ref[index, 2 - b, d] = acc[index, at:at + channels, :channels]
            for k in range(1, ns):
                rs_copy(k).wait_send()
                ag_copy(k).wait_send()
            for k in range(1, nz):
                z_copy(k).wait_send()

        return scatter, across, gather, finish

    steps = [reduction(tap) for tap in range(3)]
    scatter, across, gather, finish = range(4)

    halo_wait(OWN)
    process(OWN)
    add_x(2)
    steps[2][scatter]()
    pl.when(j == 0)(add_g0)
    pl.when(j == 1)(add_g1)
    clear()

    has_n1 = j < last
    passes_on = j < last

    def c1_row(r):
        @pl.when(j >= 2)
        def _():
            own_c1(r).wait_recv()
            pl.when(passes_on)(lambda: fwd_c1(r).start())

    def halo_after(slot, r):
        if r == 0:
            halo_start_up(slot)
        if r == rows - 1:
            halo_start_down(slot)

    c1_row(order[0])
    for count, r in enumerate(order):
        @pl.when(j >= 1)
        def _():
            own_c0(r).wait_recv()
            pl.when(passes_on)(lambda: fwd_c0(r).start())
            halo_after(C0, r)

        @pl.when(has_n1)
        def _():
            to_prev(r).wait_recv()
            pl.when(j >= 1)(lambda: fwd_prev(r).start())
            halo_after(N1, r)

        if count == 1:
            steps[2][across]()
        if count == 2:
            steps[2][gather]()

    @pl.when(j == 1)
    def _():
        for r in order[1:]:
            own_c1(r).start()

    @pl.when(has_n1)
    def _():
        halo_wait(N1)
        process(N1)
        add_x(1)
        pl.when(j == 0)(add_g1)
        clear()

    c1_row(order[1])

    @pl.when(j >= 1)
    def _():
        halo_wait(C0)
        process(C0)
        add_g0()
        clear()

    steps[1][scatter]()
    for r in order[2:-1]:
        c1_row(r)

    def late_row(r):
        row_copy(FWD_PREV, N1, late, r, prev).wait_recv()

    for r in order[:-1]:
        @pl.when(j < last - 1)
        def _():
            late_row(r)

        halo_after(late, r)
    missing = order[-1] + 1
    halo_wait(late)
    run(functools.partial(shift_row, late), 0, missing)
    run(functools.partial(shift_row, late), missing + 1, rows + 2)
    run(functools.partial(compute_row, late), 0, missing - 2)
    steps[1][across]()
    c1_row(order[-1])

    @pl.when(j < last - 1)
    def _():
        late_row(order[-1])

    shift_row(late, missing)
    run(functools.partial(compute_row, late), missing - 2, rows)
    pl.when(j < last - 1)(lambda: add_x(0))
    pl.when(j >= last - 1)(add_g1)
    steps[0][scatter]()
    steps[1][gather]()
    for h in range(rows):
        ig_ref[h] = dacc[h, :channels, :].astype(jnp.bfloat16)
        cg_ref[0, h] = dacc[h, channels:channels + share, :].astype(jnp.bfloat16)
        cg_ref[1, h] = dacc[h, high:high + share, :].astype(jnp.bfloat16)
    steps[2][finish]()
    steps[0][across]()
    steps[1][finish]()
    steps[0][gather]()

    for r in range(rows):
        @pl.when(j >= 1)
        def _():
            to_prev(r).wait_send()

        @pl.when(jnp.logical_and(j >= 1, has_n1))
        def _():
            fwd_prev(r).wait_send()

        @pl.when(j == 0)
        def _():
            own_c0(r).wait_send()

        @pl.when(j == 1)
        def _():
            own_c1(r).wait_send()

        @pl.when(jnp.logical_and(j >= 1, passes_on))
        def _():
            fwd_c0(r).wait_send()

        @pl.when(jnp.logical_and(j >= 2, passes_on))
        def _():
            fwd_c1(r).wait_send()
    steps[0][finish]()


def up_to(value, step):
    return -(-value // step) * step


def per_device(nz, ns, frames, cache, grad_out, weight):
    j = lax.axis_index("tm")
    _, channels, rows, cols = frames.shape
    share = cache.shape[1]
    taps = 9 * channels
    stack = 128 + up_to(share, 32)
    ck = up_to(-(-taps // ns), 16)
    g = jnp.transpose(grad_out[0], (1, 0, 2))
    x = jnp.transpose(frames[0], (1, 0, 2))
    c = jnp.transpose(cache, (0, 2, 1, 3))
    wt = jnp.transpose(weight[:, ::-1], (0, 4, 1, 2, 3)).reshape(3, channels, taps)
    wc = lax.dynamic_slice_in_dim(wt[:2], j * share, share, axis=1)
    scale = 1.0 / math.sqrt(nz * ns * rows * cols)
    f32, bf16 = jnp.float32, jnp.bfloat16
    vmem = pl.BlockSpec(memory_space=pltpu.VMEM)
    dma = pltpu.SemaphoreType.DMA
    ig, cg, weight_grad = pl.pallas_call(
        functools.partial(kernel, nz, ns, ck, channels, share, scale),
        out_shape=(
            jax.ShapeDtypeStruct((rows, channels, cols), bf16),
            jax.ShapeDtypeStruct((2, rows, share, cols), bf16),
            jax.ShapeDtypeStruct(weight.shape, f32),
        ),
        in_specs=[vmem] * 5,
        out_specs=(vmem,) * 3,
        scratch_shapes=[
            pltpu.VMEM((5, rows + 2, channels, cols), bf16),
            pltpu.VMEM(((rows + 2) * 3 * channels, cols), bf16),
            pltpu.VMEM((rows, stack, cols), f32),
            pltpu.VMEM((taps, 256), f32),
            pltpu.VMEM((3, ns * ck, 128), f32),
            pltpu.VMEM((rows, stack, cols), bf16),
            pltpu.VMEM((5, stack, taps), bf16),
            pltpu.VMEM((3, ns, ck, 128), bf16), pltpu.VMEM((3, ns, ck, 128), bf16),
            pltpu.VMEM((3, ck, 128), bf16), pltpu.VMEM((3, nz, ck, 128), bf16),
            pltpu.VMEM((3, ns, ck, 128), bf16),
            dma((5, rows)), dma((5, rows)), dma((5, 2)), dma((5, 2)),
            dma((3, ns)), dma((3, ns)), dma((3, nz)), dma((3, nz)), dma((3, ns)), dma((3, ns)),
        ],
        compiler_params=pltpu.CompilerParams(
            collective_id=0, has_side_effects=True, vmem_limit_bytes=60 * 1024 * 1024),
    )(g, x, c, wt, wc)
    return (jnp.transpose(ig, (1, 0, 2))[None], jnp.transpose(cg, (0, 2, 1, 3)), weight_grad)


def solution(mesh):
    placed = (
        P("tm", None, "space", None),
        P(None, "tm", "space", None),
        P("tm", None, "space", None),
        P(),
    )
    return jax.shard_map(
        functools.partial(per_device, mesh.shape["tm"], mesh.shape["space"]),
        mesh=mesh,
        in_specs=placed,
        out_specs=(P("tm", None, "space", None), P(None, "tm", "space", None), P()),
        check_vma=False,
    )
```

time: 128 us -> 113 us (0.88); the launches traced: 126 us -> 112 us
  local copies, waits for them, and re-layouts: 17.6 us -> 11.2 us
  Pallas kernels: 105 us -> 101 us
  other arithmetic: 2.48 us -> 0 us
    pallas_call x1, Pallas kernels: 105 us -> 101 us  [per_device(): pl.pallas_call(functools.partial(kernel, nz, ns, ck, channels, share, sca...]
    unnamed x45 -> x15, local copies, waits for them, and re-layouts: 12.2 us -> 8.4 us
    slice x7 -> x1, local copies, waits for them, and re-layouts: 2.82 us -> 0.03 us  [per_device(): wc = lax.dynamic_slice_in_dim(wt[:2], j * share, share, axis=1)]
    concatenate x6 -> x0, local copies, waits for them, and re-layouts: 1.82 us -> none  [stacked(): return jnp.concatenate(parts, axis=dim)]
    transpose x0 -> x1, local copies, waits for them, and re-layouts: none -> 1.46 us  [per_device(): x = jnp.transpose(frames[0], (1, 0, 2))]
where the time goes in v2:
time: 113 us; the launch traced here: 112 us
  Pallas kernels  101 us (89%)
  local copies, waits for them, and re-layouts  11.2 us (10%)
    pallas_call x1, Pallas kernels, per_device(): pl.pallas_call(functools.partial(kernel, nz, ns, ck, channels, share, sca...  101 us
    unnamed x15, local copies, waits for them, and re-layouts  8.4 us

profile of v2, /device:TPU:0, one launch (start us, length us, event | category | flops | bytes accessed | tf_op | source)
XLA Modules:
  0.0 112.5 jit_solution(1013383696223836680)
XLA Ops:
  0.6 0.0 copy-start
  0.6 1.9 %copy.25 = bf16[2,24,4,1280]{3,1,2,0:T(8,128)(2,1)} copy(bf16[2,24,4,1280]{3,2,1,0:T(4,128)(2,1)} %param.5) | data formatting | bytes 983040 | tf_op args[1]
  2.6 0.0 copy-done
  2.7 0.2 constant_dynamic-slice_fusion
  2.9 0.8 copy.21.wc_ref
  3.7 0.0 copy-start.2
  3.7 0.0 copy-start.3
  3.7 1.1 copy.18.wt_ref
  4.8 0.1 copy-done.2
  4.9 0.5 copy-done.3
  5.4 1.5 %copy_bitcast_fusion = (bf16[4,96,1280]{2,1,0:T(8,128)(2,1)}, bf16[4,96,1280]{2,1,0:T(8,128)(2,1)}) fusion(bf16[1,96,4,1280]{3,2,1,0:T(4,128)(2,1)S(1)} %copy-done.2, bf16[1,96,4,1280]{3,2,1,0:T(4,128)(2,1)S(1)} %copy-done.3), kind=kLoop, calls=%fused_computation | loop fusion | bytes 3932160 | tf_op jit(solution)/shard_map/transpose | solution.py:434
  6.8 100.5 %shard_map.67 = (bf16[4,96,1280]{2,1,0:T(8,128)(2,1)}, bf16[2,4,24,1280]{3,2,1,0:T(8,128)(2,1)}, f32[3,3,3,96,96]{4,3,2,1,0:T(8,128)}) custom-call(bf16[4,96,1280]{2,1,0:T(8,128)(2,1)} %get-tuple-element.16.g_ref, bf16[4,96,1280]{2,1,0:T(8,128)(2,1)} %get-tuple-element.15.x_ref, bf16[2,4,24,1280]{3,2,1,0:T(8,128)(2,1)} %bitcast.21, ...), custom_call_target="tpu_custom_call" | custom-call | tf_op jit(solution)/shard_map/pallas_call | solution.py:442
  107.4 0.0 copy-start.4
  107.4 0.0 copy-start.1
  107.4 3.0 %copy.19 = bf16[1,96,4,1280]{3,2,1,0:T(4,128)(2,1)} copy(bf16[1,96,4,1280]{3,1,2,0:T(8,128)(2,1)} %bitcast.23) | data formatting | bytes 1966080
  110.4 0.0 copy-done.4
  110.4 1.0 copy.20
  111.4 0.0 copy-done.1
  111.4 1.1 copy.27
  (3 shorter events, 0.1 us)
Async XLA Ops:
  0.6 1.9 %copy-start = (bf16[3,3,3,96,96]{4,3,2,1,0:T(8,128)(2,1)S(1)}, bf16[3,3,3,96,96]{4,3,2,1,0:T(8,128)(2,1)}, u32[]{:S(2)}) copy-start(bf16[3,3,3,96,96]{4,3,2,1,0:T(8,128)(2,1)} %param.7) | copy-start | bytes 1492996
  3.7 1.2 %copy-start.2 = (bf16[1,96,4,1280]{3,2,1,0:T(4,128)(2,1)S(1)}, bf16[1,96,4,1280]{3,2,1,0:T(4,128)(2,1)}, u32[]{:S(2)}) copy-start(bf16[1,96,4,1280]{3,2,1,0:T(4,128)(2,1)} %param.4) | copy-start | bytes 2949124
  3.7 1.7 %copy-start.3 = (bf16[1,96,4,1280]{3,2,1,0:T(4,128)(2,1)S(1)}, bf16[1,96,4,1280]{3,2,1,0:T(4,128)(2,1)}, u32[]{:S(2)}) copy-start(bf16[1,96,4,1280]{3,2,1,0:T(4,128)(2,1)} %param.6) | copy-start | bytes 2949124
  107.4 3.1 %copy-start.4 = (bf16[2,4,24,1280]{3,2,1,0:T(8,128)(2,1)S(1)}, bf16[2,4,24,1280]{3,2,1,0:T(8,128)(2,1)}, u32[]{:S(2)}) copy-start(bf16[2,4,24,1280]{3,2,1,0:T(8,128)(2,1)} %get-tuple-element.7) | copy-start | bytes 1474564
  107.4 4.0 %copy-start.1 = (f32[3,3,3,96,96]{4,3,2,1,0:T(8,128)S(1)}, f32[3,3,3,96,96]{4,3,2,1,0:T(8,128)}, u32[]{:S(2)}) copy-start(f32[3,3,3,96,96]{4,3,2,1,0:T(8,128)} %get-tuple-element.22) | copy-start | bytes 2985988

commit v3 on v2

--- a/solution.py
+++ b/solution.py
@@ -14,7 +14,7 @@
 
 
 def kernel(
-    nz, ns, ck, channels, share, scale,
+    nz, ns, ck, channels, share,
     g_ref, x_ref, c_ref, wt_ref, wc_ref, ig_ref, cg_ref, wg_ref,
     gp, sc, dacc, wtmp, acc, xs_ref, wl_ref,
     sb, rb, zs, zb, gb,
@@ -264,7 +264,7 @@
             total = zb[index, 0].astype(jnp.float32)
             for q in range(1, nz):
                 total = total + zb[index, q].astype(jnp.float32)
-            gb[index, s] = (total * scale).astype(jnp.bfloat16)
+            gb[index, s] = total.astype(jnp.bfloat16)
             for k in range(1, ns):
                 ag_copy(k).start()
 
@@ -288,6 +288,28 @@
     steps = [reduction(tap) for tap in range(3)]
     scatter, across, gather, finish = range(4)
 
+    has_n1 = j < last
+    passes_on = j < last
+
+    def c1_row(r):
+        @pl.when(j >= 2)
+        def _():
+            own_c1(r).wait_recv()
+            pl.when(passes_on)(lambda: fwd_c1(r).start())
+
+    def halo_after(slot, r):
+        if r == 0:
+            halo_start_up(slot)
+        if r == rows - 1:
+            halo_start_down(slot)
+
+    def c0_row(r):
+        own_c0(r).wait_recv()
+        pl.when(passes_on)(lambda: fwd_c0(r).start())
+        halo_after(C0, r)
+
+    c1_row(order[0])
+    pl.when(j == 1)(lambda: c0_row(order[0]))
     halo_wait(OWN)
     process(OWN)
     add_x(2)
@@ -296,28 +318,8 @@
     pl.when(j == 1)(add_g1)
     clear()
 
-    has_n1 = j < last
-    passes_on = j < last
-
-    def c1_row(r):
-        @pl.when(j >= 2)
-        def _():
-            own_c1(r).wait_recv()
-            pl.when(passes_on)(lambda: fwd_c1(r).start())
-
-    def halo_after(slot, r):
-        if r == 0:
-            halo_start_up(slot)
-        if r == rows - 1:
-            halo_start_down(slot)
-
-    c1_row(order[0])
     for count, r in enumerate(order):
-        @pl.when(j >= 1)
-        def _():
-            own_c0(r).wait_recv()
-            pl.when(passes_on)(lambda: fwd_c0(r).start())
-            halo_after(C0, r)
+        pl.when(j >= (2 if count == 0 else 1))(lambda: c0_row(r))
 
         @pl.when(has_n1)
         def _():
@@ -325,10 +327,6 @@
             pl.when(j >= 1)(lambda: fwd_prev(r).start())
             halo_after(N1, r)
 
-        if count == 1:
-            steps[2][across]()
-        if count == 2:
-            steps[2][gather]()
 
     @pl.when(j == 1)
     def _():
@@ -370,8 +368,9 @@
     run(functools.partial(shift_row, late), 0, missing)
     run(functools.partial(shift_row, late), missing + 1, rows + 2)
     run(functools.partial(compute_row, late), 0, missing - 2)
+    c1_row(order[-1])
+    steps[2][across]()
     steps[1][across]()
-    c1_row(order[-1])
 
     @pl.when(j < last - 1)
     def _():
@@ -382,13 +381,14 @@
     pl.when(j < last - 1)(lambda: add_x(0))
     pl.when(j >= last - 1)(add_g1)
     steps[0][scatter]()
+    steps[2][gather]()
     steps[1][gather]()
     for h in range(rows):
         ig_ref[h] = dacc[h, :channels, :].astype(jnp.bfloat16)
         cg_ref[0, h] = dacc[h, channels:channels + share, :].astype(jnp.bfloat16)
         cg_ref[1, h] = dacc[h, high:high + share, :].astype(jnp.bfloat16)
+    steps[0][across]()
     steps[2][finish]()
-    steps[0][across]()
     steps[1][finish]()
     steps[0][gather]()
 
@@ -440,7 +440,7 @@
     vmem = pl.BlockSpec(memory_space=pltpu.VMEM)
     dma = pltpu.SemaphoreType.DMA
     ig, cg, weight_grad = pl.pallas_call(
-        functools.partial(kernel, nz, ns, ck, channels, share, scale),
+        functools.partial(kernel, nz, ns, ck, channels, share),
         out_shape=(
             jax.ShapeDtypeStruct((rows, channels, cols), bf16),
             jax.ShapeDtypeStruct((2, rows, share, cols), bf16),
@@ -465,7 +465,7 @@
         compiler_params=pltpu.CompilerParams(
             collective_id=0, has_side_effects=True, vmem_limit_bytes=60 * 1024 * 1024),
     )(g, x, c, wt, wc)
-    return (jnp.transpose(ig, (1, 0, 2))[None], jnp.transpose(cg, (0, 2, 1, 3)), weight_grad)
+    return (jnp.transpose(ig, (1, 0, 2))[None], jnp.transpose(cg, (0, 2, 1, 3)), weight_grad * scale)
 
 
 def solution(mesh):

time: 113 us -> 99 us (0.88)
  Pallas kernels: 101 us -> 86.8 us
  other arithmetic: 0 us -> 1.18 us
    pallas_call x1, Pallas kernels: 101 us -> 86.8 us  [per_device(): pl.pallas_call(functools.partial(kernel, nz, ns, ck, channels, share), ou...]
    mul x0 -> x1, other arithmetic: none -> 1.18 us  [per_device(): weight_grad * scale]
    unnamed x15 -> x14, local copies, waits for them, and re-layouts: 8.4 us -> 7.34 us
where the time goes in v3:
time: 99 us; the launch traced here: 98.8 us
  Pallas kernels  86.8 us (88%)
  local copies, waits for them, and re-layouts  10.2 us (10%)
  other arithmetic  1.18 us (1%)
    pallas_call x1, Pallas kernels, per_device(): pl.pallas_call(functools.partial(kernel, nz, ns, ck, channels, share), ou...  86.8 us
    unnamed x14, local copies, waits for them, and re-layouts  7.34 us

profile of v3, /device:TPU:0, one launch (start us, length us, event | category | flops | bytes accessed | tf_op | source)
XLA Modules:
  0.0 98.8 jit_solution(16636803604905877843)
XLA Ops:
  0.6 0.0 copy-start
  0.6 1.9 %copy.25 = bf16[2,24,4,1280]{3,1,2,0:T(8,128)(2,1)} copy(bf16[2,24,4,1280]{3,2,1,0:T(4,128)(2,1)} %param.5) | data formatting | bytes 983040 | tf_op args[1]
  2.6 0.0 copy-done
  2.7 0.2 constant_dynamic-slice_fusion
  2.9 0.8 copy.21.wc_ref
  3.7 0.0 copy-start.2
  3.7 0.0 copy-start.3
  3.7 1.1 %copy.18.wt_ref = bf16[3,96,864]{2,1,0:T(8,128)(2,1)} copy(bf16[3,96,864]{1,2,0:T(8,128)(2,1)S(1)} %bitcast.20) | data formatting | bytes 995328 | tf_op jit(solution)/shard_map/reshape | solution.py:436
  4.8 0.1 copy-done.2
  4.9 0.5 copy-done.3
  5.4 1.5 %copy_bitcast_fusion = (bf16[4,96,1280]{2,1,0:T(8,128)(2,1)}, bf16[4,96,1280]{2,1,0:T(8,128)(2,1)}) fusion(bf16[1,96,4,1280]{3,2,1,0:T(4,128)(2,1)S(1)} %copy-done.2, bf16[1,96,4,1280]{3,2,1,0:T(4,128)(2,1)S(1)} %copy-done.3), kind=kLoop, calls=%fused_computation | loop fusion | bytes 3932160 | tf_op jit(solution)/shard_map/transpose | solution.py:434
  6.8 86.8 %shard_map.67 = (bf16[4,96,1280]{2,1,0:T(8,128)(2,1)}, bf16[2,4,24,1280]{3,2,1,0:T(8,128)(2,1)}, f32[3,3,3,96,96]{4,3,2,1,0:T(8,128)}) custom-call(bf16[4,96,1280]{2,1,0:T(8,128)(2,1)} %get-tuple-element.16.g_ref, bf16[4,96,1280]{2,1,0:T(8,128)(2,1)} %get-tuple-element.15.x_ref, bf16[2,4,24,1280]{3,2,1,0:T(8,128)(2,1)} %bitcast.21, ...), custom_call_target="tpu_custom_call" | custom-call | tf_op jit(solution)/shard_map/pallas_call | solution.py:442
  93.6 0.0 copy-start.4
  93.6 0.0 copy-start.1
  93.6 3.0 %copy.19 = bf16[1,96,4,1280]{3,2,1,0:T(4,128)(2,1)} copy(bf16[1,96,4,1280]{3,1,2,0:T(8,128)(2,1)} %bitcast.23) | data formatting | bytes 1966080
  96.7 0.0 copy-done.4
  96.7 1.0 copy.20
  97.6 0.0 copy-done.1
  97.6 1.2 %broadcast_multiply_fusion = f32[3,3,3,96,96]{4,3,2,1,0:T(8,128)} fusion(f32[3,3,3,96,96]{4,3,2,1,0:T(8,128)S(1)} %copy-done.1), kind=kLoop, calls=%fused_computation.2 | loop fusion | flops 248832 | bytes 1990656 | tf_op jit(solution)/shard_map/mul | solution.py:468
  (3 shorter events, 0.1 us)
Async XLA Ops:
  0.6 1.9 %copy-start = (bf16[3,3,3,96,96]{4,3,2,1,0:T(8,128)(2,1)S(1)}, bf16[3,3,3,96,96]{4,3,2,1,0:T(8,128)(2,1)}, u32[]{:S(2)}) copy-start(bf16[3,3,3,96,96]{4,3,2,1,0:T(8,128)(2,1)} %param.7) | copy-start | bytes 1492996
  3.7 1.2 %copy-start.2 = (bf16[1,96,4,1280]{3,2,1,0:T(4,128)(2,1)S(1)}, bf16[1,96,4,1280]{3,2,1,0:T(4,128)(2,1)}, u32[]{:S(2)}) copy-start(bf16[1,96,4,1280]{3,2,1,0:T(4,128)(2,1)} %param.4) | copy-start | bytes 2949124
  3.7 1.7 %copy-start.3 = (bf16[1,96,4,1280]{3,2,1,0:T(4,128)(2,1)S(1)}, bf16[1,96,4,1280]{3,2,1,0:T(4,128)(2,1)}, u32[]{:S(2)}) copy-start(bf16[1,96,4,1280]{3,2,1,0:T(4,128)(2,1)} %param.6) | copy-start | bytes 2949124
  93.6 3.1 %copy-start.4 = (bf16[2,4,24,1280]{3,2,1,0:T(8,128)(2,1)S(1)}, bf16[2,4,24,1280]{3,2,1,0:T(8,128)(2,1)}, u32[]{:S(2)}) copy-start(bf16[2,4,24,1280]{3,2,1,0:T(8,128)(2,1)} %get-tuple-element.7) | copy-start | bytes 1474564
  93.6 4.0 %copy-start.1 = (f32[3,3,3,96,96]{4,3,2,1,0:T(8,128)S(1)}, f32[3,3,3,96,96]{4,3,2,1,0:T(8,128)}, u32[]{:S(2)}) copy-start(f32[3,3,3,96,96]{4,3,2,1,0:T(8,128)} %get-tuple-element.8) | copy-start | bytes 2985988
